TPU v7x, 32 devices: a whole 2x2x4 slice. The times are simulated.
32 devices in a mesh: tm: 4 (over z), row: 2 (over core), col: 4 (over y, x).
Axes of the slice: x: 2, y: 2, z: 4, core: 2. Of those that a mesh axis runs over, the one named last changes fastest.
Arguments:
- features: bfloat16 [8, 32, 128, 128], P('tm', 'row', 'col'), may hold values from -65 to 65
- conv_first: bfloat16 [3, 3, 3, 128, 128], replicated, may hold values from -0.109375 to 0.109375
- conv_second: bfloat16 [3, 3, 3, 128, 128], replicated, may hold values from -0.109375 to 0.109375
- out_grad: bfloat16 [8, 32, 128, 128], P('tm', 'row', 'col'), may hold values from -6 to 6
Outputs:
- result: bfloat16 [8, 32, 128, 128], P('tm', 'row', 'col')
- feature_grad: bfloat16 [8, 32, 128, 128], P('tm', 'row', 'col')
- first_grad: bfloat16 [3, 3, 3, 128, 128], replicated
- second_grad: bfloat16 [3, 3, 3, 128, 128], replicated
All inputs are finite; a program needn't handle non-finite values.
Results may differ from a plain program's by a relative error of at most 0.0068.
Values may be sent and summed in bfloat16 or wider, within the bound.
No kernel may reach another device: no remote copies, remote signals or barrier semaphores. Data moves between devices by JAX's collectives and lax.ppermute only.
A program may use at most 64 MiB of HBM per device.

v0:
```python
import math
import jax
import jax.numpy as jnp
from jax import lax
from jax.sharding import PartitionSpec as P

GROUPS = 32
EPSILON = 1e-06
NUMBERS = ("NDHWC", "DHWIO", "NDHWC")
SWAPPED = ("CDHWN", "DHWIO", "CDHWN")


def extended(cells, sides, width):
    for axis, dim in sides:
        count = lax.axis_size(axis)
        ends = count - 1
        head = lax.slice_in_dim(cells, 0, width, axis=dim)
        tail = lax.slice_in_dim(cells, cells.shape[dim] - width, cells.shape[dim], axis=dim)
        cells = jnp.concatenate(
            [
                lax.ppermute(tail, axis, [(i, (i + 1) % count) for i in range(ends)]),
                cells,
                lax.ppermute(head, axis, [((i + 1) % count, i) for i in range(ends)]),
            ],
            axis=dim,
        )
    return cells


def passed_along(shard, axis, by):
    peers = lax.axis_size(axis)
    pairs = [(i, i + by) for i in range(peers) if 0 <= i + by < peers]
    return lax.ppermute(shard, axis, pairs)


def conv_valid(window, kernel):
    return lax.conv_general_dilated(
        window[None],
        kernel,
        (1, 1, 1),
        "VALID",
        dimension_numbers=NUMBERS,
        preferred_element_type=jnp.float32,
    )[0]


def flipped(kernel):
    return jnp.transpose(jnp.flip(kernel, (0, 1, 2)), (0, 1, 2, 4, 3))


def window(values, step):
    rimmed = extended(values, (("row", 1), ("col", 2)), 1)
    if step > 0:
        piece = rimmed[-2:]
    else:
        piece = rimmed[:2]
    neighbour = passed_along(piece, "tm", step)
    if step > 0:
        return jnp.concatenate([neighbour, rimmed], 0)
    return jnp.concatenate([rimmed, neighbour], 0)


def group_sum(values):
    per_group = values.shape[3] // GROUPS
    return values.sum((1, 2)).reshape(values.shape[0], GROUPS, per_group).sum(2)


def widen(stat, per_group):
    return jnp.repeat(stat, per_group, axis=1)[:, None, None, :]


def tile_count(values):
    return (
        values.shape[1]
        * values.shape[2]
        * lax.axis_size("row")
        * lax.axis_size("col")
        * (values.shape[3] // GROUPS)
    )


def norm_act(raw):
    values = raw.astype(jnp.float32)
    per_group = values.shape[3] // GROUPS
    count = tile_count(values)
    group_mean = lax.psum(group_sum(values), ("row", "col")) / count
    centred = values - widen(group_mean, per_group)
    spread = lax.psum(group_sum(centred * centred), ("row", "col")) / count
    inv_std = widen(lax.rsqrt(spread + EPSILON), per_group)
    normed = centred * inv_std
    return ((normed * jax.nn.sigmoid(normed)).astype(jnp.bfloat16), normed, inv_std)


def norm_back(grad_act, normed, inv_std):
    per_group = normed.shape[3] // GROUPS
    count = tile_count(normed)
    sigmoid_z = jax.nn.sigmoid(normed)
    grad_norm = grad_act * sigmoid_z * (1.0 + normed * (1.0 - sigmoid_z))
    first_total, second_total = lax.psum(
        (group_sum(grad_norm), group_sum(grad_norm * normed)), ("row", "col")
    )
    first_mean = widen(first_total / count, per_group)
    second_mean = widen(second_total / count, per_group)
    return inv_std * (grad_norm - first_mean - normed * second_mean)


def weight_grad(padded, grad):
    summed = lax.conv_general_dilated(
        padded[None],
        grad[:, :, :, None, :],
        (1, 1, 1),
        "VALID",
        dimension_numbers=SWAPPED,
        preferred_element_type=jnp.float32,
    )
    return jnp.transpose(summed, (1, 2, 3, 4, 0))


def on_device(features, conv_first, conv_second, out_grad):
    cells = (
        features.shape[0]
        * features.shape[1]
        * features.shape[2]
        * lax.axis_size("tm")
        * lax.axis_size("row")
        * lax.axis_size("col")
    )
    factor = 1.0 / math.sqrt(cells)
    act_first, norm_first, std_first = norm_act(features)
    pad_first = window(act_first, 1)
    hidden = conv_valid(pad_first, conv_first).astype(jnp.bfloat16)
    act_second, norm_second, std_second = norm_act(hidden)
    pad_second = window(act_second, 1)
    branch = conv_valid(pad_second, conv_second)
    result = (features.astype(jnp.float32) + branch).astype(jnp.bfloat16)
    grad_window = window(out_grad, -1)
    second_term = weight_grad(pad_second, out_grad)
    grad_act2 = conv_valid(grad_window, flipped(conv_second))
    hidden_grad = norm_back(grad_act2, norm_second, std_second).astype(jnp.bfloat16)
    hidden_window = window(hidden_grad, -1)
    grad_act1 = conv_valid(hidden_window, flipped(conv_first))
    first_term = weight_grad(pad_first, hidden_grad)
    feature_grad = (
        out_grad.astype(jnp.float32) + norm_back(grad_act1, norm_first, std_first)
    ).astype(jnp.bfloat16)
    first_total, second_total = lax.psum((first_term, second_term), ("tm", "row", "col"))
    first_grad = (first_total * factor).astype(jnp.bfloat16)
    second_grad = (second_total * factor).astype(jnp.bfloat16)
    return (result, feature_grad, first_grad, second_grad)


def solution(mesh):
    in_specs = (P("tm", "row", "col", None), P(), P(), P("tm", "row", "col", None))
    out_specs = (P("tm", "row", "col", None), P("tm", "row", "col", None), P(), P())
    return jax.shard_map(
        on_device, mesh=mesh, in_specs=in_specs, out_specs=out_specs, check_vma=False
    )
```

profile of v0, /device:TPU:0, one launch (start us, length us, event | category | flops | bytes accessed | tf_op | source)
XLA Modules:
  0.0 334.4 jit_solution(3689381599951502855)
XLA Ops:
  8.6 15.8 %psum.70 = f32[2,32]{1,0:T(2,128)S(1)} all-reduce(f32[2,32]{1,0:T(2,128)S(1)} %reduce_sum.145), channel_id=1, replica_groups=mesh['tm'=4,'row'=2,'col'=4] {'row','col'}, use_global_device_ids=true, to_apply=%region_2.0 | all-reduce | flops 64 | bytes 512 | tf_op jit(solution)/shard_map/psum | solution.py:86
  25.8 14.2 %psum.71 = f32[2,32]{1,0:T(2,128)S(1)} all-reduce(f32[2,32]{1,0:T(2,128)S(1)} %reduce_sum.147), channel_id=1, replica_groups=mesh['tm'=4,'row'=2,'col'=4] {'row','col'}, use_global_device_ids=true, to_apply=%region_5.0 | all-reduce | flops 64 | bytes 512 | tf_op jit(solution)/shard_map/psum | solution.py:88
  43.3 3.0 collective-permute-start
  51.0 4.8 %collective-permute-start.2 = (bf16[2,18,1,128]{3,1,2,0:T(8,128)(2,1)S(1)}, bf16[2,18,1,128]{3,1,2,0:T(8,128)(2,1)S(1)}, u32[]{:S(2)}, u32[]{:S(2)}) collective-permute-start(bf16[2,18,1,128]{3,1,2,0:T(8,128)(2,1)S(1)} %get-tuple-element.30), channel_id=1, source_target_pairs={{0,1},{1,2},{2,3},{4,5},{5,6},{6,7},{8,9},{9,10},{10,11},{12,13},{... | collective-permute-start | bytes 27656 | tf_op jit(solution)/shard_map/ppermute | solution.py:21
  57.4 3.5 %collective-permute-start.4 = (bf16[2,18,34,128]{3,1,2,0:T(8,128)(2,1)S(1)}, bf16[2,18,34,128]{3,1,2,0:T(8,128)(2,1)S(1)}, u32[]{:S(2)}, u32[]{:S(2)}) collective-permute-start(bf16[2,18,34,128]{3,1,2,0:T(8,128)(2,1)S(1)} %pad_maximum_fusion), channel_id=1, source_target_pairs={{0,8},{8,16},{16,24},{1,9},{9,17},{17,25},{2,10},{10,18},{18,26},{... | collective-permute-start | bytes 940040 | tf_op jit(solution)/shard_map/ppermute | solution.py:33
  62.2 5.4 %collective-permute-start.12 = (bf16[2,18,1,128]{3,2,1,0:T(2,128)(2,1)S(1)}, bf16[2,18,1,128]{3,2,1,0:T(2,128)(2,1)S(1)}, u32[]{:S(2)}, u32[]{:S(2)}) collective-permute-start(bf16[2,18,1,128]{3,2,1,0:T(2,128)(2,1)S(1)} %get-tuple-element.32), channel_id=1, source_target_pairs={{0,1},{1,2},{2,3},{4,5},{5,6},{6,7},{8,9},{9,10},{10,11},{12,13},{... | collective-permute-start | bytes 27656 | tf_op jit(solution)/shard_map/ppermute | solution.py:21
  72.5 2.5 select_reduce_fusion
  75.3 17.4 %psum.72 = f32[2,32]{1,0:T(2,128)S(1)} all-reduce(f32[2,32]{1,0:T(2,128)S(1)} %reduce_sum.149), channel_id=1, replica_groups=mesh['tm'=4,'row'=2,'col'=4] {'row','col'}, use_global_device_ids=true, to_apply=%region_8.0 | all-reduce | flops 64 | bytes 512 | tf_op jit(solution)/shard_map/psum | solution.py:86
  93.1 14.5 %psum.73 = f32[2,32]{1,0:T(2,128)S(1)} all-reduce(f32[2,32]{1,0:T(2,128)S(1)} %reduce_sum.151), channel_id=1, replica_groups=mesh['tm'=4,'row'=2,'col'=4] {'row','col'}, use_global_device_ids=true, to_apply=%region_11.0 | all-reduce | flops 64 | bytes 512 | tf_op jit(solution)/shard_map/psum | solution.py:88
  109.5 2.5 convolution_select_fusion.1
  112.8 14.7 %all-reduce.2 = (f32[2,32]{1,0:T(2,128)S(1)}, f32[2,32]{1,0:T(2,128)S(1)}) all-reduce(f32[2,32]{1,0:T(2,128)S(1)} %reduce_sum.155, f32[2,32]{1,0:T(2,128)S(1)} %reduce_sum.153), channel_id=1, replica_groups=mesh['tm'=4,'row'=2,'col'=4] {'row','col'}, use_global_device_ids=true, to_apply=%region_17.18 | all-reduce | flops 128 | bytes 1024 | tf_op jit(solution)/shard_map/psum | solution.py:99
  129.7 3.0 collective-permute-start.15
  134.1 3.0 collective-permute-start.5
  139.3 4.5 %collective-permute-start.7 = (bf16[2,18,1,128]{3,1,2,0:T(8,128)(2,1)S(1)}, bf16[2,18,1,128]{3,1,2,0:T(8,128)(2,1)S(1)}, u32[]{:S(2)}, u32[]{:S(2)}) collective-permute-start(bf16[2,18,1,128]{3,1,2,0:T(8,128)(2,1)S(1)} %get-tuple-element.28), channel_id=1, source_target_pairs={{0,1},{1,2},{2,3},{4,5},{5,6},{6,7},{8,9},{9,10},{10,11},{12,13},{... | collective-permute-start | bytes 27656 | tf_op jit(solution)/shard_map/ppermute | solution.py:21
  145.8 5.8 %collective-permute-start.17 = (bf16[2,18,1,128]{3,1,2,0:T(8,128)(2,1)}, bf16[2,18,1,128]{3,1,2,0:T(8,128)(2,1)}, u32[]{:S(2)}, u32[]{:S(2)}) collective-permute-start(bf16[2,18,1,128]{3,1,2,0:T(8,128)(2,1)} %get-tuple-element.26), channel_id=1, source_target_pairs={{0,1},{1,2},{2,3},{4,5},{5,6},{6,7},{8,9},{9,10},{10,11},{12,13},{... | collective-permute-start | bytes 27656 | tf_op jit(solution)/shard_map/ppermute | solution.py:21
  152.6 5.5 %collective-permute-start.9 = (bf16[2,18,34,128]{3,1,2,0:T(8,128)(2,1)}, bf16[2,18,34,128]{3,1,2,0:T(8,128)(2,1)}, u32[]{:S(2)}, u32[]{:S(2)}) collective-permute-start(bf16[2,18,34,128]{3,1,2,0:T(8,128)(2,1)} %pad_maximum_fusion.1), channel_id=1, source_target_pairs={{0,8},{8,16},{16,24},{1,9},{9,17},{17,25},{2,10},{10,18},{18,26},{... | collective-permute-start | bytes 940040 | tf_op jit(solution)/shard_map/ppermute | solution.py:33
  158.1 9.0 %fusion.6 = f32[3,3,3,128,128]{4,3,2,1,0:T(8,128)} fusion(bf16[1,4,18,34,128]{4,2,3,1,0:T(8,128)(2,1)S(1)} %copy-done.11, bf16[2,16,32,1,128]{4,1,2,0,3:T(8,128)(2,1)S(1)} %fusion.67), kind=kOutput, calls=%fused_computation.9 | convolution fusion | flops 905969664 | bytes 2658304 | tf_op jit(solution)/shard_map/transpose | solution.py:116
  170.5 2.3 fusion.89
  172.8 9.0 %fusion.4 = f32[3,3,3,128,128]{4,3,2,1,0:T(8,128)} fusion(bf16[1,4,18,34,128]{4,2,3,1,0:T(8,128)(2,1)S(1)} %get-tuple-element.20, bf16[2,16,32,1,128]{4,2,1,0,3:T(8,128)(2,1)S(1)} %bitcast.93), kind=kOutput, calls=%fused_computation.7 | convolution fusion | flops 905969664 | bytes 2658304 | tf_op jit(solution)/shard_map/transpose | solution.py:116
  184.7 2.5 convolution_select_fusion
  188.1 15.5 %all-reduce.1 = (f32[2,32]{1,0:T(2,128)S(1)}, f32[2,32]{1,0:T(2,128)S(1)}) all-reduce(f32[2,32]{1,0:T(2,128)S(1)} %reduce_sum.159, f32[2,32]{1,0:T(2,128)S(1)} %reduce_sum.157), channel_id=1, replica_groups=mesh['tm'=4,'row'=2,'col'=4] {'row','col'}, use_global_device_ids=true, to_apply=%region_23.24 | all-reduce | flops 128 | bytes 1024 | tf_op jit(solution)/shard_map/psum | solution.py:99
  205.2 2.5 convolution_select_fusion.2
  209.6 114.0 %all-reduce.5.cloned.1.call-done = (f32[3,3,3,128,128]{4,3,2,1,0:T(8,128)}, f32[3,3,3,128,128]{4,3,2,1,0:T(8,128)}) async-done(((f32[3,3,3,128,128]{4,3,2,1,0:T(8,128)}, f32[3,3,3,128,128]{4,3,2,1,0:T(8,128)}), (f32[3,3,3,128,128]{4,3,2,1,0:T(8,128)}, f32[3,3,3,128,128]{4,3,2,1,0:T(8,128)})) %all-reduce.5.cloned.1.call-update) | async-done | bytes 3538960 | tf_op jit(solution)/shard_map/psum | solution.py:146
  323.6 2.8 multiply_convert_fusion.1
  (176 shorter events, 41.8 us)
Async XLA Ops:
  7.2 65.1 %copy-start = (bf16[3,3,3,128,128]{4,3,2,1,0:T(8,128)(2,1)S(1)}, bf16[3,3,3,128,128]{4,3,2,1,0:T(8,128)(2,1)}, u32[]{:S(2)}) copy-start(bf16[3,3,3,128,128]{4,3,2,1,0:T(8,128)(2,1)} %param.5) | copy-start | bytes 2654212
  7.2 48.6 %copy-start.9 = (bf16[2,16,32,128]{3,2,1,0:T(8,128)(2,1)S(1)}, bf16[2,16,32,128]{3,2,1,0:T(8,128)(2,1)}, u32[]{:S(2)}) copy-start(bf16[2,16,32,128]{3,2,1,0:T(8,128)(2,1)} %param.7) | copy-start | bytes 786436
  7.2 316.4 %all-reduce.5.cloned.1.call-start = ((), (), s32[]{:S(2)}) async-start(), calls=%async_computation | async-start | bytes 7077888 | tf_op jit(solution)/shard_map/psum | solution.py:146
  42.0 7.7 %collective-permute-start.1 = (bf16[2,1,32,128]{3,1,2,0:T(2,128)(2,1)S(1)}, bf16[2,1,32,128]{3,1,2,0:T(2,128)(2,1)S(1)}, u32[]{:S(2)}, u32[]{:S(2)}) collective-permute-start(bf16[2,1,32,128]{3,1,2,0:T(2,128)(2,1)S(1)} %get-tuple-element.43), channel_id=1, source_target_pairs={{4,0},{5,1},{6,2},{7,3},{12,8},{13,9},{14,10},{15,11},{20,16},{21,... | collective-permute-start | bytes 49160 | tf_op jit(solution)/shard_map/ppermute | solution.py:23
  43.3 6.4 %collective-permute-start = (bf16[2,1,32,128]{3,1,2,0:T(2,128)(2,1)S(1)}, bf16[2,1,32,128]{3,1,2,0:T(2,128)(2,1)S(1)}, u32[]{:S(2)}, u32[]{:S(2)}) collective-permute-start(bf16[2,1,32,128]{3,1,2,0:T(2,128)(2,1)S(1)} %get-tuple-element.42), channel_id=1, source_target_pairs={{0,4},{1,5},{2,6},{3,7},{8,12},{9,13},{10,14},{11,15},{16,20},{17,... | collective-permute-start | bytes 49160 | tf_op jit(solution)/shard_map/ppermute | solution.py:21
  47.0 8.8 %collective-permute-start.10 = (bf16[2,1,32,128]{3,2,1,0:T(8,128)(2,1)S(1)}, bf16[2,1,32,128]{3,2,1,0:T(8,128)(2,1)S(1)}, u32[]{:S(2)}, u32[]{:S(2)}) collective-permute-start(bf16[2,1,32,128]{3,2,1,0:T(8,128)(2,1)S(1)} %get-tuple-element.39), channel_id=1, source_target_pairs={{0,4},{1,5},{2,6},{3,7},{8,12},{9,13},{10,14},{11,15},{16,20},{17,... | collective-permute-start | bytes 49160 | tf_op jit(solution)/shard_map/ppermute | solution.py:21
  48.3 7.5 %collective-permute-start.11 = (bf16[2,1,32,128]{3,2,1,0:T(8,128)(2,1)S(1)}, bf16[2,1,32,128]{3,2,1,0:T(8,128)(2,1)S(1)}, u32[]{:S(2)}, u32[]{:S(2)}) collective-permute-start(bf16[2,1,32,128]{3,2,1,0:T(8,128)(2,1)S(1)} %get-tuple-element.38), channel_id=1, source_target_pairs={{4,0},{5,1},{6,2},{7,3},{12,8},{13,9},{14,10},{15,11},{20,16},{21,... | collective-permute-start | bytes 49160 | tf_op jit(solution)/shard_map/ppermute | solution.py:23
  49.7 6.2 %collective-permute-start.3 = (bf16[2,18,1,128]{3,1,2,0:T(8,128)(2,1)S(1)}, bf16[2,18,1,128]{3,1,2,0:T(8,128)(2,1)S(1)}, u32[]{:S(2)}, u32[]{:S(2)}) collective-permute-start(bf16[2,18,1,128]{3,1,2,0:T(8,128)(2,1)S(1)} %get-tuple-element.31), channel_id=1, source_target_pairs={{1,0},{2,1},{3,2},{5,4},{6,5},{7,6},{9,8},{10,9},{11,10},{13,12},{... | collective-permute-start | bytes 27656 | tf_op jit(solution)/shard_map/ppermute | solution.py:23
  51.0 6.2 %collective-permute-start.2 = (bf16[2,18,1,128]{3,1,2,0:T(8,128)(2,1)S(1)}, bf16[2,18,1,128]{3,1,2,0:T(8,128)(2,1)S(1)}, u32[]{:S(2)}, u32[]{:S(2)}) collective-permute-start(bf16[2,18,1,128]{3,1,2,0:T(8,128)(2,1)S(1)} %get-tuple-element.30), channel_id=1, source_target_pairs={{0,1},{1,2},{2,3},{4,5},{5,6},{6,7},{8,9},{9,10},{10,11},{12,13},{... | collective-permute-start | bytes 27656 | tf_op jit(solution)/shard_map/ppermute | solution.py:21
  57.4 13.2 %collective-permute-start.4 = (bf16[2,18,34,128]{3,1,2,0:T(8,128)(2,1)S(1)}, bf16[2,18,34,128]{3,1,2,0:T(8,128)(2,1)S(1)}, u32[]{:S(2)}, u32[]{:S(2)}) collective-permute-start(bf16[2,18,34,128]{3,1,2,0:T(8,128)(2,1)S(1)} %pad_maximum_fusion), channel_id=1, source_target_pairs={{0,8},{8,16},{16,24},{1,9},{9,17},{17,25},{2,10},{10,18},{18,26},{... | collective-permute-start | bytes 940040 | tf_op jit(solution)/shard_map/ppermute | solution.py:33
  60.9 6.8 %collective-permute-start.13 = (bf16[2,18,1,128]{3,2,1,0:T(2,128)(2,1)S(1)}, bf16[2,18,1,128]{3,2,1,0:T(2,128)(2,1)S(1)}, u32[]{:S(2)}, u32[]{:S(2)}) collective-permute-start(bf16[2,18,1,128]{3,2,1,0:T(2,128)(2,1)S(1)} %get-tuple-element.33), channel_id=1, source_target_pairs={{1,0},{2,1},{3,2},{5,4},{6,5},{7,6},{9,8},{10,9},{11,10},{13,12},{... | collective-permute-start | bytes 27656 | tf_op jit(solution)/shard_map/ppermute | solution.py:23
  62.2 6.9 %collective-permute-start.12 = (bf16[2,18,1,128]{3,2,1,0:T(2,128)(2,1)S(1)}, bf16[2,18,1,128]{3,2,1,0:T(2,128)(2,1)S(1)}, u32[]{:S(2)}, u32[]{:S(2)}) collective-permute-start(bf16[2,18,1,128]{3,2,1,0:T(2,128)(2,1)S(1)} %get-tuple-element.32), channel_id=1, source_target_pairs={{0,1},{1,2},{2,3},{4,5},{5,6},{6,7},{8,9},{9,10},{10,11},{12,13},{... | collective-permute-start | bytes 27656 | tf_op jit(solution)/shard_map/ppermute | solution.py:21
  69.3 38.5 %collective-permute-start.14 = (bf16[2,18,34,128]{3,2,1,0:T(8,128)(2,1)S(1)}, bf16[2,18,34,128]{3,2,1,0:T(8,128)(2,1)S(1)}, u32[]{:S(2)}, u32[]{:S(2)}) collective-permute-start(bf16[2,18,34,128]{3,2,1,0:T(8,128)(2,1)S(1)} %pad_maximum_fusion.3), channel_id=1, source_target_pairs={{8,0},{16,8},{24,16},{9,1},{17,9},{25,17},{10,2},{18,10},{26,18},{... | collective-permute-start | bytes 940040 | tf_op jit(solution)/shard_map/ppermute | solution.py:33
  128.2 29.9 %copy-start.5 = (bf16[2,16,32,128]{3,1,2,0:T(8,128)(2,1)}, bf16[2,16,32,128]{3,1,2,0:T(8,128)(2,1)S(1)}, u32[]{:S(2)}) copy-start(bf16[2,16,32,128]{3,1,2,0:T(8,128)(2,1)S(1)} %get-tuple-element.25) | copy-start | bytes 786436
  128.3 15.6 %collective-permute-start.16 = (bf16[2,1,32,128]{3,1,2,0:T(2,128)(2,1)S(1)}, bf16[2,1,32,128]{3,1,2,0:T(2,128)(2,1)S(1)}, u32[]{:S(2)}, u32[]{:S(2)}) collective-permute-start(bf16[2,1,32,128]{3,1,2,0:T(2,128)(2,1)S(1)} %get-tuple-element.37), channel_id=1, source_target_pairs={{4,0},{5,1},{6,2},{7,3},{12,8},{13,9},{14,10},{15,11},{20,16},{21,... | collective-permute-start | bytes 49160 | tf_op jit(solution)/shard_map/ppermute | solution.py:23
  129.7 14.2 %collective-permute-start.15 = (bf16[2,1,32,128]{3,1,2,0:T(2,128)(2,1)S(1)}, bf16[2,1,32,128]{3,1,2,0:T(2,128)(2,1)S(1)}, u32[]{:S(2)}, u32[]{:S(2)}) collective-permute-start(bf16[2,1,32,128]{3,1,2,0:T(2,128)(2,1)S(1)} %get-tuple-element.36), channel_id=1, source_target_pairs={{0,4},{1,5},{2,6},{3,7},{8,12},{9,13},{10,14},{11,15},{16,20},{17,... | collective-permute-start | bytes 49160 | tf_op jit(solution)/shard_map/ppermute | solution.py:21
  132.8 4.7 %collective-permute-start.6 = (bf16[2,1,32,128]{3,1,2,0:T(2,128)(2,1)S(1)}, bf16[2,1,32,128]{3,1,2,0:T(2,128)(2,1)S(1)}, u32[]{:S(2)}, u32[]{:S(2)}) collective-permute-start(bf16[2,1,32,128]{3,1,2,0:T(2,128)(2,1)S(1)} %get-tuple-element.41), channel_id=1, source_target_pairs={{4,0},{5,1},{6,2},{7,3},{12,8},{13,9},{14,10},{15,11},{20,16},{21,... | collective-permute-start | bytes 49160 | tf_op jit(solution)/shard_map/ppermute | solution.py:23
  134.1 3.9 %collective-permute-start.5 = (bf16[2,1,32,128]{3,1,2,0:T(2,128)(2,1)S(1)}, bf16[2,1,32,128]{3,1,2,0:T(2,128)(2,1)S(1)}, u32[]{:S(2)}, u32[]{:S(2)}) collective-permute-start(bf16[2,1,32,128]{3,1,2,0:T(2,128)(2,1)S(1)} %get-tuple-element.40), channel_id=1, source_target_pairs={{0,4},{1,5},{2,6},{3,7},{8,12},{9,13},{10,14},{11,15},{16,20},{17,... | collective-permute-start | bytes 49160 | tf_op jit(solution)/shard_map/ppermute | solution.py:21
  138.0 13.6 %collective-permute-start.8 = (bf16[2,18,1,128]{3,1,2,0:T(8,128)(2,1)S(1)}, bf16[2,18,1,128]{3,1,2,0:T(8,128)(2,1)S(1)}, u32[]{:S(2)}, u32[]{:S(2)}) collective-permute-start(bf16[2,18,1,128]{3,1,2,0:T(8,128)(2,1)S(1)} %get-tuple-element.29), channel_id=1, source_target_pairs={{1,0},{2,1},{3,2},{5,4},{6,5},{7,6},{9,8},{10,9},{11,10},{13,12},{... | collective-permute-start | bytes 27656 | tf_op jit(solution)/shard_map/ppermute | solution.py:23
  139.3 12.3 %collective-permute-start.7 = (bf16[2,18,1,128]{3,1,2,0:T(8,128)(2,1)S(1)}, bf16[2,18,1,128]{3,1,2,0:T(8,128)(2,1)S(1)}, u32[]{:S(2)}, u32[]{:S(2)}) collective-permute-start(bf16[2,18,1,128]{3,1,2,0:T(8,128)(2,1)S(1)} %get-tuple-element.28), channel_id=1, source_target_pairs={{0,1},{1,2},{2,3},{4,5},{5,6},{6,7},{8,9},{9,10},{10,11},{12,13},{... | collective-permute-start | bytes 27656 | tf_op jit(solution)/shard_map/ppermute | solution.py:21
  144.5 22.6 %collective-permute-start.18 = (bf16[2,18,1,128]{3,1,2,0:T(8,128)(2,1)}, bf16[2,18,1,128]{3,1,2,0:T(8,128)(2,1)}, u32[]{:S(2)}, u32[]{:S(2)}) collective-permute-start(bf16[2,18,1,128]{3,1,2,0:T(8,128)(2,1)} %get-tuple-element.27), channel_id=1, source_target_pairs={{1,0},{2,1},{3,2},{5,4},{6,5},{7,6},{9,8},{10,9},{11,10},{13,12},{... | collective-permute-start | bytes 27656 | tf_op jit(solution)/shard_map/ppermute | solution.py:23
  145.8 21.3 %collective-permute-start.17 = (bf16[2,18,1,128]{3,1,2,0:T(8,128)(2,1)}, bf16[2,18,1,128]{3,1,2,0:T(8,128)(2,1)}, u32[]{:S(2)}, u32[]{:S(2)}) collective-permute-start(bf16[2,18,1,128]{3,1,2,0:T(8,128)(2,1)} %get-tuple-element.26), channel_id=1, source_target_pairs={{0,1},{1,2},{2,3},{4,5},{5,6},{6,7},{8,9},{9,10},{10,11},{12,13},{... | collective-permute-start | bytes 27656 | tf_op jit(solution)/shard_map/ppermute | solution.py:21
  152.6 17.9 %collective-permute-start.9 = (bf16[2,18,34,128]{3,1,2,0:T(8,128)(2,1)}, bf16[2,18,34,128]{3,1,2,0:T(8,128)(2,1)}, u32[]{:S(2)}, u32[]{:S(2)}) collective-permute-start(bf16[2,18,34,128]{3,1,2,0:T(8,128)(2,1)} %pad_maximum_fusion.1), channel_id=1, source_target_pairs={{0,8},{8,16},{16,24},{1,9},{9,17},{17,25},{2,10},{10,18},{18,26},{... | collective-permute-start | bytes 940040 | tf_op jit(solution)/shard_map/ppermute | solution.py:33
  169.0 13.0 %collective-permute-start.19 = (bf16[2,18,34,128]{3,1,2,0:T(8,128)(2,1)}, bf16[2,18,34,128]{3,1,2,0:T(8,128)(2,1)}, u32[]{:S(2)}, u32[]{:S(2)}) collective-permute-start(bf16[2,18,34,128]{3,1,2,0:T(8,128)(2,1)} %pad_maximum_fusion.2), channel_id=1, source_target_pairs={{8,0},{16,8},{24,16},{9,1},{17,9},{25,17},{10,2},{18,10},{26,18},{... | collective-permute-start | bytes 940040 | tf_op jit(solution)/shard_map/ppermute | solution.py:33
  (25 other events, 259.3 us)
Sparse Core Ops, SparseCore 0:
  181.9 141.6 all-reduce.4
where the time goes:
time: 335 us; the launch traced here: 334 us
  waiting for transfers between devices  117 us (35%)
  blocking collectives  92 us (27%)
  starting transfers between devices  53.2 us (16%)
  matrix products  27.9 us (8%)
  other arithmetic  18.4 us (5%)
  between operations  14.9 us (4%)
  local copies, waits for them, and re-layouts  10.5 us (3%)
    psum x1, waiting for transfers between devices, on_device(): lax.psum((first_term, second_term), ('tm', 'row', 'col'))  114 us
    psum x2, blocking collectives, norm_act(): group_mean = lax.psum(group_sum(values), ('row', 'col')) / count  33.1 us
    ppermute x8, starting transfers between devices, extended(): lax.ppermute(tail, axis, [(i, (i + 1) % count) for i in range(ends)])  30.9 us
    psum x2, blocking collectives, norm_back(): lax.psum((group_sum(grad_norm), group_sum(grad_norm * normed)), ('row', '...  30.2 us
    psum x2, blocking collectives, norm_act(): spread = lax.psum(group_sum(centred * centred), ('row', 'col')) / count  28.7 us
    transpose x2, matrix products, weight_grad(): return jnp.transpose(summed, (1, 2, 3, 4, 0))  18 us
    ppermute x4, starting transfers between devices, passed_along(): return lax.ppermute(shard, axis, pairs)  11.8 us
    ppermute x8, starting transfers between devices, extended(): lax.ppermute(head, axis, [((i + 1) % count, i) for i in range(ends)])  10.5 us
  transfers between devices with their start and end apart: 21, of which 5 were waited for; matrix products, arithmetic and copies ran while one was open for 12% of the time, Pallas kernels for 0%

commit v1 on v0

--- a/solution.py
+++ b/solution.py
@@ -143,7 +143,13 @@
     feature_grad = (
         out_grad.astype(jnp.float32) + norm_back(grad_act1, norm_first, std_first)
     ).astype(jnp.bfloat16)
-    first_total, second_total = lax.psum((first_term, second_term), ("tm", "row", "col"))
+
+    def run_outputs_all(xs):
+        for dev in (("row", "col"), "tm"):
+            xs = jax.lax.psum(xs, dev)
+        return xs
+
+    first_total, second_total = run_outputs_all((first_term, second_term))
     first_grad = (first_total * factor).astype(jnp.bfloat16)
     second_grad = (second_total * factor).astype(jnp.bfloat16)
     return (result, feature_grad, first_grad, second_grad)

time: 335 us -> 402 us (1.20)
  waiting for transfers between devices: 117 us -> 188 us
    psum x1 -> x2, waiting for transfers between devices: 114 us -> 150 us  [run_outputs_all(): xs = jax.lax.psum(xs, dev)]
    ppermute x4, waiting for transfers between devices: 0.16 us -> 31 us  [passed_along(): return lax.ppermute(shard, axis, pairs)]
  transfers between devices with their start and end apart: 21 -> 22, of which waited for: 5 -> 9; matrix products, arithmetic and copies ran while one was open for 12% -> 6% of each run, Pallas kernels for 0% -> 0%
where the time goes in v1:
time: 402 us; the launch traced here: 401 us
  waiting for transfers between devices  188 us (47%)
  blocking collectives  91.9 us (23%)
  starting transfers between devices  51.7 us (13%)
  matrix products  28.2 us (7%)
  other arithmetic  15.8 us (4%)
  between operations  14.8 us (4%)
  local copies, waits for them, and re-layouts  10.2 us (3%)
    psum x2, waiting for transfers between devices, run_outputs_all(): xs = jax.lax.psum(xs, dev)  150 us
    psum x2, blocking collectives, norm_act(): group_mean = lax.psum(group_sum(values), ('row', 'col')) / count  33.1 us
    ppermute x4, waiting for transfers between devices, passed_along(): return lax.ppermute(shard, axis, pairs)  31 us
    psum x2, blocking collectives, norm_back(): lax.psum((group_sum(grad_norm), group_sum(grad_norm * normed)), ('row', '...  30.1 us
    ppermute x8, starting transfers between devices, extended(): lax.ppermute(tail, axis, [(i, (i + 1) % count) for i in range(ends)])  29.7 us
    psum x2, blocking collectives, norm_act(): spread = lax.psum(group_sum(centred * centred), ('row', 'col')) / count  28.7 us
    transpose x2, matrix products, weight_grad(): return jnp.transpose(summed, (1, 2, 3, 4, 0))  18.2 us
    ppermute x4, starting transfers between devices, passed_along(): return lax.ppermute(shard, axis, pairs)  11.4 us
  transfers between devices with their start and end apart: 22, of which 9 were waited for; matrix products, arithmetic and copies ran while one was open for 6% of the time, Pallas kernels for 0%

profile of v1, /device:TPU:0, one launch (start us, length us, event | category | flops | bytes accessed | tf_op | source)
XLA Modules:
  0.0 400.7 jit_solution(509103014287984524)
XLA Ops:
  8.6 15.8 %psum.84 = f32[2,32]{1,0:T(2,128)S(1)} all-reduce(f32[2,32]{1,0:T(2,128)S(1)} %reduce_sum.145), channel_id=1, replica_groups=mesh['tm'=4,'row'=2,'col'=4] {'row','col'}, use_global_device_ids=true, to_apply=%region_2.0 | all-reduce | flops 64 | bytes 512 | tf_op jit(solution)/shard_map/psum | solution.py:86
  25.8 14.2 %psum.85 = f32[2,32]{1,0:T(2,128)S(1)} all-reduce(f32[2,32]{1,0:T(2,128)S(1)} %reduce_sum.147), channel_id=1, replica_groups=mesh['tm'=4,'row'=2,'col'=4] {'row','col'}, use_global_device_ids=true, to_apply=%region_5.0 | all-reduce | flops 64 | bytes 512 | tf_op jit(solution)/shard_map/psum | solution.py:88
  42.7 3.0 collective-permute-start
  50.4 4.8 %collective-permute-start.2 = (bf16[2,18,1,128]{3,1,2,0:T(8,128)(2,1)S(1)}, bf16[2,18,1,128]{3,1,2,0:T(8,128)(2,1)S(1)}, u32[]{:S(2)}, u32[]{:S(2)}) collective-permute-start(bf16[2,18,1,128]{3,1,2,0:T(8,128)(2,1)S(1)} %get-tuple-element.32), channel_id=1, source_target_pairs={{0,1},{1,2},{2,3},{4,5},{5,6},{6,7},{8,9},{9,10},{10,11},{12,13},{... | collective-permute-start | bytes 27656 | tf_op jit(solution)/shard_map/ppermute | solution.py:21
  56.9 3.5 collective-permute-start.4
  61.7 5.4 %collective-permute-start.12 = (bf16[2,18,1,128]{3,2,1,0:T(2,128)(2,1)S(1)}, bf16[2,18,1,128]{3,2,1,0:T(2,128)(2,1)S(1)}, u32[]{:S(2)}, u32[]{:S(2)}) collective-permute-start(bf16[2,18,1,128]{3,2,1,0:T(2,128)(2,1)S(1)} %get-tuple-element.34), channel_id=1, source_target_pairs={{0,1},{1,2},{2,3},{4,5},{5,6},{6,7},{8,9},{9,10},{10,11},{12,13},{... | collective-permute-start | bytes 27656 | tf_op jit(solution)/shard_map/ppermute | solution.py:21
  74.7 17.4 %psum.86 = f32[2,32]{1,0:T(2,128)S(1)} all-reduce(f32[2,32]{1,0:T(2,128)S(1)} %reduce_sum.149), channel_id=1, replica_groups=mesh['tm'=4,'row'=2,'col'=4] {'row','col'}, use_global_device_ids=true, to_apply=%region_8.0 | all-reduce | flops 64 | bytes 512 | tf_op jit(solution)/shard_map/psum | solution.py:86
  92.6 14.5 %psum.87 = f32[2,32]{1,0:T(2,128)S(1)} all-reduce(f32[2,32]{1,0:T(2,128)S(1)} %reduce_sum.151), channel_id=1, replica_groups=mesh['tm'=4,'row'=2,'col'=4] {'row','col'}, use_global_device_ids=true, to_apply=%region_11.0 | all-reduce | flops 64 | bytes 512 | tf_op jit(solution)/shard_map/psum | solution.py:88
  109.0 2.5 convolution_select_fusion.1
  112.3 14.7 %all-reduce.1 = (f32[2,32]{1,0:T(2,128)S(1)}, f32[2,32]{1,0:T(2,128)S(1)}) all-reduce(f32[2,32]{1,0:T(2,128)S(1)} %reduce_sum.155, f32[2,32]{1,0:T(2,128)S(1)} %reduce_sum.153), channel_id=1, replica_groups=mesh['tm'=4,'row'=2,'col'=4] {'row','col'}, use_global_device_ids=true, to_apply=%region_17.18 | all-reduce | flops 128 | bytes 1024 | tf_op jit(solution)/shard_map/psum | solution.py:99
  129.8 3.0 collective-permute-start.5
  135.0 4.5 %collective-permute-start.7 = (bf16[2,18,1,128]{3,1,2,0:T(8,128)(2,1)S(1)}, bf16[2,18,1,128]{3,1,2,0:T(8,128)(2,1)S(1)}, u32[]{:S(2)}, u32[]{:S(2)}) collective-permute-start(bf16[2,18,1,128]{3,1,2,0:T(8,128)(2,1)S(1)} %get-tuple-element.30), channel_id=1, source_target_pairs={{0,1},{1,2},{2,3},{4,5},{5,6},{6,7},{8,9},{9,10},{10,11},{12,13},{... | collective-permute-start | bytes 27656 | tf_op jit(solution)/shard_map/ppermute | solution.py:21
  141.9 5.3 %collective-permute-start.9 = (bf16[2,18,34,128]{3,1,2,0:T(8,128)(2,1)}, bf16[2,18,34,128]{3,1,2,0:T(8,128)(2,1)}, u32[]{:S(2)}, u32[]{:S(2)}) collective-permute-start(bf16[2,18,34,128]{3,1,2,0:T(8,128)(2,1)} %pad_maximum_fusion.1), channel_id=1, source_target_pairs={{0,8},{8,16},{16,24},{1,9},{9,17},{17,25},{2,10},{10,18},{18,26},{... | collective-permute-start | bytes 940040 | tf_op jit(solution)/shard_map/ppermute | solution.py:33
  147.3 9.0 %fusion.6 = f32[3,3,3,128,128]{4,3,2,1,0:T(8,128)} fusion(bf16[1,4,18,34,128]{4,2,3,1,0:T(8,128)(2,1)S(1)} %copy-done.9, bf16[2,16,32,1,128]{4,1,2,0,3:T(8,128)(2,1)S(1)} %fusion.67), kind=kOutput, calls=%fused_computation.9 | convolution fusion | flops 905969664 | bytes 2658304 | tf_op jit(solution)/shard_map/transpose | solution.py:116
  158.6 9.2 %fusion.4 = f32[3,3,3,128,128]{4,3,2,1,0:T(8,128)} fusion(bf16[1,4,18,34,128]{4,2,3,1,0:T(8,128)(2,1)S(1)} %get-tuple-element.22, bf16[2,16,32,1,128]{4,2,1,0,3:T(8,128)(2,1)S(1)} %bitcast.93), kind=kOutput, calls=%fused_computation.7 | convolution fusion | flops 905969664 | bytes 2658304 | tf_op jit(solution)/shard_map/transpose | solution.py:116
  167.9 76.5 %all-reduce.7.cloned.1.call-done = (f32[3,3,3,128,128]{4,3,2,1,0:T(8,128)}, f32[3,3,3,128,128]{4,3,2,1,0:T(8,128)}) async-done(((f32[3,3,3,128,128]{4,3,2,1,0:T(8,128)}, f32[3,3,3,128,128]{4,3,2,1,0:T(8,128)}), (f32[3,3,3,128,128]{4,3,2,1,0:T(8,128)}, f32[3,3,3,128,128]{4,3,2,1,0:T(8,128)})) %all-reduce.7.cloned.1.call-update) | async-done | bytes 3538960 | tf_op jit(solution)/shard_map/psum | solution.py:149
  246.7 3.0 collective-permute-start.15
  251.9 4.5 %collective-permute-start.17 = (bf16[2,18,1,128]{3,1,2,0:T(8,128)(2,1)S(1)}, bf16[2,18,1,128]{3,1,2,0:T(8,128)(2,1)S(1)}, u32[]{:S(2)}, u32[]{:S(2)}) collective-permute-start(bf16[2,18,1,128]{3,1,2,0:T(8,128)(2,1)S(1)} %get-tuple-element.28), channel_id=1, source_target_pairs={{0,1},{1,2},{2,3},{4,5},{5,6},{6,7},{8,9},{9,10},{10,11},{12,13},{... | collective-permute-start | bytes 27656 | tf_op jit(solution)/shard_map/ppermute | solution.py:21
  259.4 31.0 %collective-permute-done.19 = bf16[2,18,34,128]{3,1,2,0:T(8,128)(2,1)S(1)} collective-permute-done((bf16[2,18,34,128]{3,1,2,0:T(8,128)(2,1)S(1)}, bf16[2,18,34,128]{3,1,2,0:T(8,128)(2,1)S(1)}, u32[]{:S(2)}, u32[]{:S(2)}) %collective-permute-start.19) | collective-permute-done | bytes 313376 | tf_op jit(solution)/shard_map/ppermute | solution.py:33
  291.3 2.5 convolution_select_fusion
  294.7 15.3 %all-reduce = (f32[2,32]{1,0:T(2,128)S(1)}, f32[2,32]{1,0:T(2,128)S(1)}) all-reduce(f32[2,32]{1,0:T(2,128)S(1)} %reduce_sum.159, f32[2,32]{1,0:T(2,128)S(1)} %reduce_sum.157), channel_id=1, replica_groups=mesh['tm'=4,'row'=2,'col'=4] {'row','col'}, use_global_device_ids=true, to_apply=%region_23.24 | all-reduce | flops 128 | bytes 1024 | tf_op jit(solution)/shard_map/psum | solution.py:99
  311.6 2.5 convolution_select_fusion.2
  316.1 73.9 %all-reduce.9.cloned.1.call-done = (f32[3,3,3,128,128]{4,3,2,1,0:T(8,128)}, f32[3,3,3,128,128]{4,3,2,1,0:T(8,128)}) async-done(((f32[3,3,3,128,128]{4,3,2,1,0:T(8,128)}, f32[3,3,3,128,128]{4,3,2,1,0:T(8,128)}), (f32[3,3,3,128,128]{4,3,2,1,0:T(8,128)}, f32[3,3,3,128,128]{4,3,2,1,0:T(8,128)})) %all-reduce.9.cloned.1.call-update) | async-done | bytes 3538960 | tf_op jit(solution)/shard_map/psum | solution.py:149
  390.0 2.8 multiply_convert_fusion.1
  (171 shorter events, 46.9 us)
Async XLA Ops:
  7.2 64.5 %copy-start = (bf16[3,3,3,128,128]{4,3,2,1,0:T(8,128)(2,1)S(1)}, bf16[3,3,3,128,128]{4,3,2,1,0:T(8,128)(2,1)}, u32[]{:S(2)}) copy-start(bf16[3,3,3,128,128]{4,3,2,1,0:T(8,128)(2,1)} %param.5) | copy-start | bytes 2654212
  7.2 48.1 %copy-start.7 = (bf16[2,16,32,128]{3,2,1,0:T(8,128)(2,1)S(1)}, bf16[2,16,32,128]{3,2,1,0:T(8,128)(2,1)}, u32[]{:S(2)}) copy-start(bf16[2,16,32,128]{3,2,1,0:T(8,128)(2,1)} %param.7) | copy-start | bytes 786436
  7.2 237.2 %all-reduce.7.cloned.1.call-start = ((), (), s32[]{:S(2)}) async-start(), calls=%async_computation | async-start | bytes 7077888 | tf_op jit(solution)/shard_map/psum | solution.py:149
  41.4 7.7 %collective-permute-start.1 = (bf16[2,1,32,128]{3,1,2,0:T(2,128)(2,1)S(1)}, bf16[2,1,32,128]{3,1,2,0:T(2,128)(2,1)S(1)}, u32[]{:S(2)}, u32[]{:S(2)}) collective-permute-start(bf16[2,1,32,128]{3,1,2,0:T(2,128)(2,1)S(1)} %get-tuple-element.45), channel_id=1, source_target_pairs={{4,0},{5,1},{6,2},{7,3},{12,8},{13,9},{14,10},{15,11},{20,16},{21,... | collective-permute-start | bytes 49160 | tf_op jit(solution)/shard_map/ppermute | solution.py:23
  42.7 6.4 %collective-permute-start = (bf16[2,1,32,128]{3,1,2,0:T(2,128)(2,1)S(1)}, bf16[2,1,32,128]{3,1,2,0:T(2,128)(2,1)S(1)}, u32[]{:S(2)}, u32[]{:S(2)}) collective-permute-start(bf16[2,1,32,128]{3,1,2,0:T(2,128)(2,1)S(1)} %get-tuple-element.44), channel_id=1, source_target_pairs={{0,4},{1,5},{2,6},{3,7},{8,12},{9,13},{10,14},{11,15},{16,20},{17,... | collective-permute-start | bytes 49160 | tf_op jit(solution)/shard_map/ppermute | solution.py:21
  46.5 8.8 %collective-permute-start.10 = (bf16[2,1,32,128]{3,2,1,0:T(8,128)(2,1)S(1)}, bf16[2,1,32,128]{3,2,1,0:T(8,128)(2,1)S(1)}, u32[]{:S(2)}, u32[]{:S(2)}) collective-permute-start(bf16[2,1,32,128]{3,2,1,0:T(8,128)(2,1)S(1)} %get-tuple-element.41), channel_id=1, source_target_pairs={{0,4},{1,5},{2,6},{3,7},{8,12},{9,13},{10,14},{11,15},{16,20},{17,... | collective-permute-start | bytes 49160 | tf_op jit(solution)/shard_map/ppermute | solution.py:21
  47.8 7.5 %collective-permute-start.11 = (bf16[2,1,32,128]{3,2,1,0:T(8,128)(2,1)S(1)}, bf16[2,1,32,128]{3,2,1,0:T(8,128)(2,1)S(1)}, u32[]{:S(2)}, u32[]{:S(2)}) collective-permute-start(bf16[2,1,32,128]{3,2,1,0:T(8,128)(2,1)S(1)} %get-tuple-element.40), channel_id=1, source_target_pairs={{4,0},{5,1},{6,2},{7,3},{12,8},{13,9},{14,10},{15,11},{20,16},{21,... | collective-permute-start | bytes 49160 | tf_op jit(solution)/shard_map/ppermute | solution.py:23
  49.1 6.2 %collective-permute-start.3 = (bf16[2,18,1,128]{3,1,2,0:T(8,128)(2,1)S(1)}, bf16[2,18,1,128]{3,1,2,0:T(8,128)(2,1)S(1)}, u32[]{:S(2)}, u32[]{:S(2)}) collective-permute-start(bf16[2,18,1,128]{3,1,2,0:T(8,128)(2,1)S(1)} %get-tuple-element.33), channel_id=1, source_target_pairs={{1,0},{2,1},{3,2},{5,4},{6,5},{7,6},{9,8},{10,9},{11,10},{13,12},{... | collective-permute-start | bytes 27656 | tf_op jit(solution)/shard_map/ppermute | solution.py:23
  50.4 6.2 %collective-permute-start.2 = (bf16[2,18,1,128]{3,1,2,0:T(8,128)(2,1)S(1)}, bf16[2,18,1,128]{3,1,2,0:T(8,128)(2,1)S(1)}, u32[]{:S(2)}, u32[]{:S(2)}) collective-permute-start(bf16[2,18,1,128]{3,1,2,0:T(8,128)(2,1)S(1)} %get-tuple-element.32), channel_id=1, source_target_pairs={{0,1},{1,2},{2,3},{4,5},{5,6},{6,7},{8,9},{9,10},{10,11},{12,13},{... | collective-permute-start | bytes 27656 | tf_op jit(solution)/shard_map/ppermute | solution.py:21
  56.9 13.2 %collective-permute-start.4 = (bf16[2,18,34,128]{3,1,2,0:T(8,128)(2,1)S(1)}, bf16[2,18,34,128]{3,1,2,0:T(8,128)(2,1)S(1)}, u32[]{:S(2)}, u32[]{:S(2)}) collective-permute-start(bf16[2,18,34,128]{3,1,2,0:T(8,128)(2,1)S(1)} %pad_maximum_fusion), channel_id=1, source_target_pairs={{0,8},{8,16},{16,24},{1,9},{9,17},{17,25},{2,10},{10,18},{18,26},{... | collective-permute-start | bytes 940040 | tf_op jit(solution)/shard_map/ppermute | solution.py:33
  60.4 6.8 %collective-permute-start.13 = (bf16[2,18,1,128]{3,2,1,0:T(2,128)(2,1)S(1)}, bf16[2,18,1,128]{3,2,1,0:T(2,128)(2,1)S(1)}, u32[]{:S(2)}, u32[]{:S(2)}) collective-permute-start(bf16[2,18,1,128]{3,2,1,0:T(2,128)(2,1)S(1)} %get-tuple-element.35), channel_id=1, source_target_pairs={{1,0},{2,1},{3,2},{5,4},{6,5},{7,6},{9,8},{10,9},{11,10},{13,12},{... | collective-permute-start | bytes 27656 | tf_op jit(solution)/shard_map/ppermute | solution.py:23
  61.7 6.9 %collective-permute-start.12 = (bf16[2,18,1,128]{3,2,1,0:T(2,128)(2,1)S(1)}, bf16[2,18,1,128]{3,2,1,0:T(2,128)(2,1)S(1)}, u32[]{:S(2)}, u32[]{:S(2)}) collective-permute-start(bf16[2,18,1,128]{3,2,1,0:T(2,128)(2,1)S(1)} %get-tuple-element.34), channel_id=1, source_target_pairs={{0,1},{1,2},{2,3},{4,5},{5,6},{6,7},{8,9},{9,10},{10,11},{12,13},{... | collective-permute-start | bytes 27656 | tf_op jit(solution)/shard_map/ppermute | solution.py:21
  68.8 38.5 %collective-permute-start.14 = (bf16[2,18,34,128]{3,2,1,0:T(8,128)(2,1)S(1)}, bf16[2,18,34,128]{3,2,1,0:T(8,128)(2,1)S(1)}, u32[]{:S(2)}, u32[]{:S(2)}) collective-permute-start(bf16[2,18,34,128]{3,2,1,0:T(8,128)(2,1)S(1)} %pad_maximum_fusion.3), channel_id=1, source_target_pairs={{8,0},{16,8},{24,16},{9,1},{17,9},{25,17},{10,2},{18,10},{26,18},{... | collective-permute-start | bytes 940040 | tf_op jit(solution)/shard_map/ppermute | solution.py:33
  128.4 4.5 %collective-permute-start.6 = (bf16[2,1,32,128]{3,1,2,0:T(2,128)(2,1)S(1)}, bf16[2,1,32,128]{3,1,2,0:T(2,128)(2,1)S(1)}, u32[]{:S(2)}, u32[]{:S(2)}) collective-permute-start(bf16[2,1,32,128]{3,1,2,0:T(2,128)(2,1)S(1)} %get-tuple-element.43), channel_id=1, source_target_pairs={{4,0},{5,1},{6,2},{7,3},{12,8},{13,9},{14,10},{15,11},{20,16},{21,... | collective-permute-start | bytes 49160 | tf_op jit(solution)/shard_map/ppermute | solution.py:23
  129.8 3.9 collective-permute-start.5
  133.7 6.2 %collective-permute-start.8 = (bf16[2,18,1,128]{3,1,2,0:T(8,128)(2,1)S(1)}, bf16[2,18,1,128]{3,1,2,0:T(8,128)(2,1)S(1)}, u32[]{:S(2)}, u32[]{:S(2)}) collective-permute-start(bf16[2,18,1,128]{3,1,2,0:T(8,128)(2,1)S(1)} %get-tuple-element.31), channel_id=1, source_target_pairs={{1,0},{2,1},{3,2},{5,4},{6,5},{7,6},{9,8},{10,9},{11,10},{13,12},{... | collective-permute-start | bytes 27656 | tf_op jit(solution)/shard_map/ppermute | solution.py:23
  135.0 5.9 %collective-permute-start.7 = (bf16[2,18,1,128]{3,1,2,0:T(8,128)(2,1)S(1)}, bf16[2,18,1,128]{3,1,2,0:T(8,128)(2,1)S(1)}, u32[]{:S(2)}, u32[]{:S(2)}) collective-permute-start(bf16[2,18,1,128]{3,1,2,0:T(8,128)(2,1)S(1)} %get-tuple-element.30), channel_id=1, source_target_pairs={{0,1},{1,2},{2,3},{4,5},{5,6},{6,7},{8,9},{9,10},{10,11},{12,13},{... | collective-permute-start | bytes 27656 | tf_op jit(solution)/shard_map/ppermute | solution.py:21
  141.9 14.4 %collective-permute-start.9 = (bf16[2,18,34,128]{3,1,2,0:T(8,128)(2,1)}, bf16[2,18,34,128]{3,1,2,0:T(8,128)(2,1)}, u32[]{:S(2)}, u32[]{:S(2)}) collective-permute-start(bf16[2,18,34,128]{3,1,2,0:T(8,128)(2,1)} %pad_maximum_fusion.1), channel_id=1, source_target_pairs={{0,8},{8,16},{16,24},{1,9},{9,17},{17,25},{2,10},{10,18},{18,26},{... | collective-permute-start | bytes 940040 | tf_op jit(solution)/shard_map/ppermute | solution.py:33
  167.8 222.1 %all-reduce.9.cloned.1.call-start = ((), (), s32[]{:S(2)}) async-start(), calls=%async_computation.1 | async-start | bytes 7077888 | tf_op jit(solution)/shard_map/psum | solution.py:149
  245.4 4.3 %collective-permute-start.16 = (bf16[2,1,32,128]{3,1,2,0:T(2,128)(2,1)S(1)}, bf16[2,1,32,128]{3,1,2,0:T(2,128)(2,1)S(1)}, u32[]{:S(2)}, u32[]{:S(2)}) collective-permute-start(bf16[2,1,32,128]{3,1,2,0:T(2,128)(2,1)S(1)} %get-tuple-element.39), channel_id=1, source_target_pairs={{4,0},{5,1},{6,2},{7,3},{12,8},{13,9},{14,10},{15,11},{20,16},{21,... | collective-permute-start | bytes 49160 | tf_op jit(solution)/shard_map/ppermute | solution.py:23
  246.7 3.9 collective-permute-start.15
  250.6 5.9 %collective-permute-start.18 = (bf16[2,18,1,128]{3,1,2,0:T(8,128)(2,1)S(1)}, bf16[2,18,1,128]{3,1,2,0:T(8,128)(2,1)S(1)}, u32[]{:S(2)}, u32[]{:S(2)}) collective-permute-start(bf16[2,18,1,128]{3,1,2,0:T(8,128)(2,1)S(1)} %get-tuple-element.29), channel_id=1, source_target_pairs={{1,0},{2,1},{3,2},{5,4},{6,5},{7,6},{9,8},{10,9},{11,10},{13,12},{... | collective-permute-start | bytes 27656 | tf_op jit(solution)/shard_map/ppermute | solution.py:23
  251.9 5.9 %collective-permute-start.17 = (bf16[2,18,1,128]{3,1,2,0:T(8,128)(2,1)S(1)}, bf16[2,18,1,128]{3,1,2,0:T(8,128)(2,1)S(1)}, u32[]{:S(2)}, u32[]{:S(2)}) collective-permute-start(bf16[2,18,1,128]{3,1,2,0:T(8,128)(2,1)S(1)} %get-tuple-element.28), channel_id=1, source_target_pairs={{0,1},{1,2},{2,3},{4,5},{5,6},{6,7},{8,9},{9,10},{10,11},{12,13},{... | collective-permute-start | bytes 27656 | tf_op jit(solution)/shard_map/ppermute | solution.py:21
  258.1 32.3 %collective-permute-start.19 = (bf16[2,18,34,128]{3,1,2,0:T(8,128)(2,1)S(1)}, bf16[2,18,34,128]{3,1,2,0:T(8,128)(2,1)S(1)}, u32[]{:S(2)}, u32[]{:S(2)}) collective-permute-start(bf16[2,18,34,128]{3,1,2,0:T(8,128)(2,1)S(1)} %pad_maximum_fusion.2), channel_id=1, source_target_pairs={{8,0},{16,8},{24,16},{9,1},{17,9},{25,17},{10,2},{18,10},{26,18},{... | collective-permute-start | bytes 940040 | tf_op jit(solution)/shard_map/ppermute | solution.py:33
  (22 other events, 155.3 us)
Sparse Core Ops, SparseCore 0:
  167.9 76.4 all-reduce.6
  246.8 143.0 all-reduce.8
